TPU v7x, 256 devices: a whole 4x4x8 slice. The times are simulated.
256 devices in a mesh: band: 32 (over x_lo, z, core), domain: 8 (over y, x_hi).
Axes of the slice: x: 4 (x_hi: 2, x_lo: 2; x = x_hi * 2 + x_lo), y: 4, z: 8, core: 2. Of those that a mesh axis runs over, the one named last changes fastest.
Arguments:
- orbitals: float32 [512, 64, 4096], P('band', 'domain'), may hold values from -6 to 6
- previous: float32 [512, 64, 4096], P('band', 'domain'), may hold values from -6 to 6
- potential: float32 [64, 4096], P('domain'), may hold values from -3 to 3
- rotation: float32 [512, 512], P(None, 'band'), may hold values from -1 to 1
- accumulated: float32 [512, 64, 4096], P('band', 'domain'), may hold values from -6 to 6
- panel: int32 [1], replicated, may hold values from 0 to 131071
Outputs:
- filtered: float32 [512, 64, 4096], P('band', 'domain')
- rotated: float32 [512, 64, 4096], P('band', 'domain')
All inputs are finite; a program needn't handle non-finite values.
Results may differ from a plain program's by a relative error of at most 0.000059.
Values sent between devices are 32-bit elements; how exact they have to be, the bound alone decides.
No kernel may reach another device: no remote copies, remote signals or barrier semaphores. Data moves between devices by JAX's collectives and lax.ppermute only.
A program may use at most 192 MiB of HBM per device.

v0:
```python
import jax
import jax.numpy as jnp
from jax import lax
from jax.sharding import PartitionSpec as P

NX = 64
coefs = (
    -5369.0 / 1800.0,
    12.0 / 7.0,
    -15.0 / 56.0,
    10.0 / 189.0,
    -1.0 / 112.0,
    2.0 / 1925.0,
    -1.0 / 16632.0,
)


def padded_2(cells, sides, width):
    for axis, dim in sides:
        count = lax.axis_size(axis)
        head = lax.slice_in_dim(cells, 0, width, axis=dim)
        tail = lax.slice_in_dim(cells, cells.shape[dim] - width, cells.shape[dim], axis=dim)
        cells = jnp.concatenate(
            [
                lax.ppermute(tail, axis, [(i, (i + 1) % count) for i in range(count)]),
                cells,
                lax.ppermute(head, axis, [((i + 1) % count, i) for i in range(count)]),
            ],
            axis=dim,
        )
    return cells


def from_root(block, axis, owner):
    block = jnp.where(lax.axis_index(axis) == owner, block, jnp.zeros_like(block))
    return lax.psum(block, axis)


def add_panel(total, rows, block):
    flat = block.reshape(block.shape[0], -1)
    product = lax.dot_general(
        rows,
        flat,
        (((0,), (0,)), ((), ())),
        precision=lax.Precision.HIGHEST,
        preferred_element_type=jnp.float32,
    )
    return total + product.reshape(total.shape)


def shift_x(values, amount, column):
    if amount > 0:
        return jnp.where(
            column >= amount, jnp.roll(values, amount, 2), jnp.roll(values, amount - NX, 2)
        )
    return jnp.where(
        column < NX + amount, jnp.roll(values, amount, 2), jnp.roll(values, amount + NX, 2)
    )


def local(orbitals, previous, potential, rotation, accumulated, panel):
    planes = orbitals.shape[1]
    cells = orbitals.shape[2]
    column = (lax.iota(jnp.int32, cells) % NX)[None, None, :]
    padded = padded_2(orbitals, (("domain", 1),), 6)
    lap = 3.0 * coefs[0] * orbitals
    for step in range(1, 7):
        lap = lap + coefs[step] * (
            padded[:, 6 + step : 6 + step + planes] + padded[:, 6 - step : 6 - step + planes]
        )
        lap = lap + coefs[step] * (
            jnp.roll(orbitals, step * NX, 2) + jnp.roll(orbitals, -step * NX, 2)
        )
        lap = lap + coefs[step] * (
            shift_x(orbitals, step, column) + shift_x(orbitals, -step, column)
        )
    ham = -2.0 * lap + potential[None] * orbitals
    filtered = (ham - 36.0 * orbitals) / 14.0 - previous
    orb_count = orbitals.shape[0]
    pairs = lax.axis_size("band") // 2
    first_root = 2 * (panel[0] % pairs)
    rows = lax.dynamic_slice_in_dim(rotation, first_root * orb_count, 2 * orb_count, 0)
    rotated = accumulated
    for member in range(2):
        block = from_root(filtered, "band", first_root + member)
        rotated = add_panel(rotated, rows[member * orb_count : (member + 1) * orb_count], block)
    return (filtered, rotated)


def solution(mesh):
    in_specs = (
        P("band", "domain", None),
        P("band", "domain", None),
        P("domain", None),
        P(None, "band"),
        P("band", "domain", None),
        P(),
    )
    out_specs = (P("band", "domain", None), P("band", "domain", None))
    return jax.shard_map(local, mesh=mesh, in_specs=in_specs, out_specs=out_specs, check_vma=False)
```

profile of v0, /device:TPU:1, one launch (start us, length us, event | category | flops | bytes accessed | tf_op | source)
XLA Modules:
  0.0 378.5 jit_solution(5414941456583426457)
XLA Ops:
  7.2 0.0 copy-start
  7.2 0.0 all-reduce.3.cloned.1.call-start
  7.2 2.6 fusion.106
  9.9 2.1 copy.22
  12.0 6.0 %collective-permute-start = (f32[16,6,4096]{2,0,1:T(8,128)}, f32[16,6,4096]{2,0,1:T(8,128)}, u32[]{:S(2)}, u32[]{:S(2)}) collective-permute-start(f32[16,6,4096]{2,0,1:T(8,128)} %copy.22), channel_id=1, source_target_pairs={{1,0},{2,1},{3,2},{4,3},{5,4},{6,5},{7,6},{0,7},{9,8},{10,9},{11,1... | collective-permute-start | bytes 4718600 | tf_op jit(solution)/shard_map/ppermute | solution.py:27
  18.0 2.1 copy.23
  20.1 0.0 collective-permute-start.1
  20.1 0.0 copy-done.1
  20.1 2.7 fusion.77
  22.8 2.7 fusion.79
  25.5 2.7 fusion.80
  28.2 2.8 fusion.85
  31.1 2.7 fusion.86
  33.7 2.7 fusion.91
  36.4 2.7 fusion.92
  39.1 2.8 fusion.97
  41.9 2.7 fusion.98
  44.5 2.7 fusion.103
  47.2 2.7 fusion.104
  49.9 2.8 fusion.110
  52.7 2.7 fusion.111
  55.4 2.2 fusion.83
  57.7 2.7 fusion.89
  60.3 2.2 fusion.95
  62.5 2.5 fusion.101
  65.0 0.1 fusion.100
  65.2 0.7 fusion.88
  65.8 0.7 fusion.94
  66.6 0.6 fusion.76
  67.2 0.7 fusion.78
  67.9 0.7 fusion.81
  68.6 0.7 fusion.82
  69.3 0.7 fusion.84
  70.0 0.7 fusion.87
  70.7 0.7 fusion.90
  71.4 0.7 fusion.93
  72.1 0.7 fusion.96
  72.8 0.7 fusion.99
  73.5 0.7 fusion.102
  74.2 0.7 fusion.105
  75.0 0.7 fusion.109
  75.7 0.7 fusion.112
  76.5 0.6 fusion.70
  77.8 0.1 constant_dynamic-update-slice_fusion
  77.9 2.1 fusion.108
  80.0 6.0 %collective-permute-done.1 = f32[16,6,4096]{2,0,1:T(8,128)} collective-permute-done((f32[16,6,4096]{2,0,1:T(8,128)}, f32[16,6,4096]{2,0,1:T(8,128)}, u32[]{:S(2)}, u32[]{:S(2)}) %collective-permute-start.1) | collective-permute-done | bytes 1572896 | tf_op jit(solution)/shard_map/ppermute | solution.py:25
  86.0 2.7 copy.17
  88.8 0.0 copy-start.3
  88.8 0.0 collective-permute-done
  88.8 2.5 copy_dynamic-update-slice_fusion
  91.3 0.0 copy-done.4
  91.3 0.0 copy-done.3
  91.3 26.4 %broadcast_select_fusion = (f32[16,8,4096]{2,1,0:T(8,128)S(1)}, f32[16,8,4096]{2,1,0:T(8,128)S(1)}) fusion(pred[]{:T(512)S(6)} %eq.11, f32[16,8,4096]{2,1,0:T(8,128)} %param.7, f32[16,8,4096]{2,1,0:T(8,128)S(1)} %copy-done.1, f32[8,4096]{1,0:T(8,128)} %param.8, f32[16,8,4038]{2,1,0:T(8,128)} %get-tuple-element.83, f32[16,8,58]{2,1,0:T(8,128)} %get-tuple-element.85, ...), kind=kLoop, calls=%fused_computation.92 | loop fusion | flops 61341696 | bytes 98222080 | tf_op jit(solution)/shard_map/jit(_where)/select_n | solution.py:35
  117.7 0.0 copy-start.2
  117.7 0.2 broadcast_select_fusion.1
  117.9 1.1 copy-done.2
  119.0 2.5 copy_bitcast_fusion.1
  121.6 2.6 copy_bitcast_fusion
  124.1 0.0 all-reduce.3.cloned.1.call-update
  124.2 237.6 %all-reduce.3.cloned.1.call-done = (f32[8,4096,16]{1,2,0:T(8,128)}, f32[8,4096,16]{1,2,0:T(8,128)}) async-done(((f32[8,4096,16]{1,2,0:T(8,128)}, f32[8,4096,16]{1,2,0:T(8,128)}), (f32[8,4096,16]{1,2,0:T(8,128)}, f32[8,4096,16]{1,2,0:T(8,128)})) %all-reduce.3.cloned.1.call-update) | async-done | bytes 4194320 | tf_op jit(solution)/shard_map/psum | solution.py:36
  361.8 0.0 copy-done
  361.8 5.3 %convolution_add_fusion.1 = f32[16,8,4096]{2,0,1:T(8,128)S(1)} fusion(f32[8,4096,16]{1,2,0:T(8,128)} %get-tuple-element.8, f32[16,8,4096]{2,1,0:T(8,128)} %param.10, f32[512,16]{0,1:T(8,128)S(1)} %copy-done, s32[]{:T(128)S(6)} %select_n.140), kind=kOutput, calls=%fused_computation.11 | convolution fusion | flops 101187584 | bytes 6299652 | tf_op jit(solution)/shard_map/dot_general | solution.py:41
  367.1 2.0 convolution_add_fusion
  369.2 2.5 copy.21
  (10 shorter events, 0.1 us)
Async XLA Ops:
  7.2 354.7 %copy-start = (f32[512,16]{0,1:T(8,128)S(1)}, f32[512,16]{0,1:T(8,128)}, u32[]{:S(2)}) copy-start(f32[512,16]{0,1:T(8,128)} %param.9) | copy-start | bytes 98308
  7.2 354.6 %all-reduce.3.cloned.1.call-start = ((), (), s32[]{:S(2)}) async-start(), calls=%async_computation | async-start | bytes 8388608 | tf_op jit(solution)/shard_map/psum | solution.py:36
  12.0 8.1 %copy-start.1 = (f32[16,8,4096]{2,1,0:T(8,128)S(1)}, f32[16,8,4096]{2,1,0:T(8,128)}, u32[]{:S(2)}) copy-start(f32[16,8,4096]{2,1,0:T(8,128)} %param.6) | copy-start | bytes 6291460
  12.0 76.8 %collective-permute-start = (f32[16,6,4096]{2,0,1:T(8,128)}, f32[16,6,4096]{2,0,1:T(8,128)}, u32[]{:S(2)}, u32[]{:S(2)}) collective-permute-start(f32[16,6,4096]{2,0,1:T(8,128)} %copy.22), channel_id=1, source_target_pairs={{1,0},{2,1},{3,2},{4,3},{5,4},{6,5},{7,6},{0,7},{9,8},{10,9},{11,1... | collective-permute-start | bytes 4718600 | tf_op jit(solution)/shard_map/ppermute | solution.py:27
  20.1 66.0 %collective-permute-start.1 = (f32[16,6,4096]{2,0,1:T(8,128)}, f32[16,6,4096]{2,0,1:T(8,128)}, u32[]{:S(2)}, u32[]{:S(2)}) collective-permute-start(f32[16,6,4096]{2,0,1:T(8,128)} %copy.23), channel_id=1, source_target_pairs={{0,1},{1,2},{2,3},{3,4},{4,5},{5,6},{6,7},{7,0},{8,9},{9,10},{10,1... | collective-permute-start | bytes 4718600 | tf_op jit(solution)/shard_map/ppermute | solution.py:25
  86.0 5.3 %copy-start.4 = (f32[16,8,4032]{2,1,0:T(8,128)S(1)}, f32[16,8,4032]{2,1,0:T(8,128)}, u32[]{:S(2)}) copy-start(f32[16,8,4032]{2,1,0:T(8,128)} %get-tuple-element.15) | copy-start | bytes 6193156
  88.8 2.5 copy-start.3
  117.7 1.3 copy-start.2
  361.8 5.3 %copy-start.5 = (f32[8,4096,16]{1,2,0:T(8,128)S(1)}, f32[8,4096,16]{1,2,0:T(8,128)}, u32[]{:S(2)}) copy-start(f32[8,4096,16]{1,2,0:T(8,128)} %get-tuple-element.9) | copy-start | bytes 6291460
Sparse Core Ops, SparseCore 0:
  124.3 237.4 all-reduce.2
where the time goes:
time: 379 us
  waiting for transfers between devices  244 us (64%)
  local copies, waits for them, and re-layouts  79.4 us (21%)
  other arithmetic  27.2 us (7%)
  between operations  14.9 us (4%)
  matrix products  7.3 us (2%)
  starting transfers between devices  6.05 us (2%)
    psum x1, waiting for transfers between devices, from_root(): return lax.psum(block, axis)  238 us
    select_n x2, other arithmetic, from_root(): jnp.where(lax.axis_index(axis) == owner, block, jnp.zeros_like(block))  26.6 us
    slice x12, local copies, waits for them, and re-layouts, shift_x(): jnp.roll(values, amount, 2)  20.7 us
    slice x12, local copies, waits for them, and re-layouts, shift_x(): jnp.roll(values, amount - NX, 2)  20.5 us
    slice x12, local copies, waits for them, and re-layouts, local(): jnp.roll(orbitals, step * NX, 2) + jnp.roll(orbitals, -step * NX, 2)  17.2 us
    unnamed x16, local copies, waits for them, and re-layouts  8.03 us
  transfers between devices with their start and end apart: 3, of which 2 were waited for; matrix products, arithmetic and copies ran while one was open for 17% of the time, Pallas kernels for 0%

commit v1 on v0

--- a/solution.py
+++ b/solution.py
@@ -33,7 +33,7 @@
 
 def from_root(block, axis, owner):
     block = jnp.where(lax.axis_index(axis) == owner, block, jnp.zeros_like(block))
-    return lax.psum(block, axis)
+    return jnp.sum(lax.all_gather(block, axis), axis=0)
 
 
 def add_panel(total, rows, block):

time: 379 us -> 872 us (2.30)
  waiting for transfers between devices: 244 us -> 695 us
  other arithmetic: 27.2 us -> 72.6 us
    all_gather x0 -> x2, waiting for transfers between devices: none -> 687 us  [from_root(): return jnp.sum(lax.all_gather(block, axis), axis=0)]
    psum x1 -> x0, waiting for transfers between devices: 238 us -> none  [from_root(): return lax.psum(block, axis)]
    reduce_sum x0 -> x2, other arithmetic: none -> 44.2 us  [from_root(): return jnp.sum(lax.all_gather(block, axis), axis=0)]
  transfers between devices with their start and end apart: 3 -> 4, of which waited for: 2 -> 3; matrix products, arithmetic and copies ran while one was open for 17% -> 10% of each run, Pallas kernels for 0% -> 0%
where the time goes in v1:
time: 872 us
  waiting for transfers between devices  695 us (80%)
  local copies, waits for them, and re-layouts  73.8 us (8%)
  other arithmetic  72.6 us (8%)
  between operations  15.3 us (2%)
    all_gather x2, waiting for transfers between devices, from_root(): return jnp.sum(lax.all_gather(block, axis), axis=0)  687 us
    reduce_sum x2, other arithmetic, from_root(): return jnp.sum(lax.all_gather(block, axis), axis=0)  44.2 us
    select_n x2, other arithmetic, from_root(): jnp.where(lax.axis_index(axis) == owner, block, jnp.zeros_like(block))  28.4 us
    slice x12, local copies, waits for them, and re-layouts, shift_x(): jnp.roll(values, amount, 2)  21 us
    slice x12, local copies, waits for them, and re-layouts, shift_x(): jnp.roll(values, amount - NX, 2)  20.7 us
  transfers between devices with their start and end apart: 4, of which 3 were waited for; matrix products, arithmetic and copies ran while one was open for 10% of the time, Pallas kernels for 0%

profile of v1, /device:TPU:1, one launch (start us, length us, event | category | flops | bytes accessed | tf_op | source)
XLA Modules:
  0.0 871.6 jit_solution(9605664045906528280)
XLA Ops:
  7.2 0.0 copy-start
  7.2 0.0 all-gather.5.cloned.1.call-start
  7.2 2.5 fusion.110
  9.8 2.1 copy.22
  11.8 6.0 collective-permute-start
  17.8 2.1 copy.23
  19.9 0.0 collective-permute-start.1
  19.9 0.0 copy-done.1
  20.0 2.7 fusion.81
  22.7 2.7 fusion.83
  25.4 2.7 fusion.84
  28.1 2.9 fusion.89
  31.0 2.7 fusion.90
  33.7 2.8 fusion.95
  36.5 2.8 fusion.96
  39.3 2.8 fusion.101
  42.1 2.7 fusion.102
  44.8 2.8 fusion.107
  47.6 2.8 fusion.108
  50.4 2.8 fusion.114
  53.2 2.8 fusion.115
  55.9 2.2 fusion.87
  58.1 2.7 fusion.93
  60.8 2.2 fusion.99
  63.0 2.5 fusion.105
  65.6 0.1 fusion.104
  65.7 0.1 fusion.92
  65.8 0.6 fusion.80
  66.5 0.7 fusion.82
  67.2 0.7 fusion.85
  67.9 0.6 fusion.86
  68.5 0.7 fusion.88
  69.2 0.7 fusion.91
  69.9 0.7 fusion.94
  70.6 0.7 fusion.97
  71.3 0.7 fusion.100
  72.1 0.7 fusion.103
  72.8 0.7 fusion.106
  73.5 0.7 fusion.109
  74.2 0.7 fusion.113
  74.9 0.7 fusion.116
  76.4 0.2 constant_dynamic-update-slice_fusion
  76.6 2.1 fusion.112
  78.7 7.2 collective-permute-done.1
  85.9 2.7 copy.17
  88.6 0.0 copy-start.4
  88.6 0.0 copy-start.6
  88.7 0.0 copy-start.7
  88.9 0.0 collective-permute-done
  88.9 2.5 copy_dynamic-update-slice_fusion
  91.7 26.9 %broadcast_select_fusion = (f32[16,8,4096]{2,1,0:T(8,128)}, f32[16,8,4096]{2,1,0:T(8,128)S(1)}) fusion(pred[]{:T(512)S(6)} %eq.11, f32[16,8,4096]{2,1,0:T(8,128)} %param.7, f32[16,8,4096]{2,1,0:T(8,128)S(1)} %copy-done.1, f32[8,4096]{1,0:T(8,128)} %param.8, f32[16,8,4038]{2,1,0:T(8,128)} %get-tuple-element.81, f32[16,8,58]{2,1,0:T(8,128)} %get-tuple-element.83, ...), kind=kLoop, calls=%fused_computation.94 | loop fusion | flops 61341696 | bytes 98222080 | tf_op jit(solution)/shard_map/jit(_where)/select_n | solution.py:35
  118.6 0.0 copy-start.2
  118.6 1.3 copy-done.2
  119.9 1.5 broadcast_select_fusion.1
  121.4 0.0 all-gather.5.cloned.1.call-update
  121.4 0.0 all-gather.7.cloned.1.call-start
  121.4 0.7 all-gather.7.cloned.1.call-update
  122.1 354.2 %all-gather.5.cloned.1.call-done = f32[512,8,4096]{2,1,0:T(8,128)} async-done(((f32[16,8,4096]{2,1,0:T(8,128)}), f32[512,8,4096]{2,1,0:T(8,128)}) %all-gather.5.cloned.1.call-update) | async-done | bytes 67108880 | tf_op jit(solution)/shard_map/all_gather | solution.py:36
  476.4 22.1 %reduce_sum.18 = f32[16,8,4096]{2,1,0:T(8,128)S(1)} reduce(f32[32,16,8,4096]{3,2,1,0:T(8,128)} %bitcast.2, f32[]{:T(128)} %constant.87.clone.1), dimensions={0}, to_apply=%region_0.1 | reduce | flops 16252928 | bytes 69206016 | tf_op jit(solution)/shard_map/reduce_sum | solution.py:36
  498.5 333.2 %all-gather.7.cloned.1.call-done = f32[512,8,4096]{2,1,0:T(8,128)} async-done(((f32[16,8,4096]{2,1,0:T(8,128)}), f32[512,8,4096]{2,1,0:T(8,128)}) %all-gather.7.cloned.1.call-update) | async-done | bytes 67108880 | tf_op jit(solution)/shard_map/all_gather | solution.py:36
  831.7 22.1 %reduce_sum.19 = f32[16,8,4096]{2,1,0:T(8,128)} reduce(f32[32,16,8,4096]{3,2,1,0:T(8,128)} %bitcast.5, f32[]{:T(128)} %constant.87.clone.1), dimensions={0}, to_apply=%region_1.2 | reduce | flops 16252928 | bytes 69206016 | tf_op jit(solution)/shard_map/reduce_sum | solution.py:36
  853.7 5.6 convolution_add_fusion.1
  859.4 2.9 convolution_add_fusion
  862.3 2.5 copy.21
  (63 shorter events, 0.2 us)
Async XLA Ops:
  7.2 846.6 %copy-start = (f32[512,16]{0,1:T(8,128)S(1)}, f32[512,16]{0,1:T(8,128)}, u32[]{:S(2)}) copy-start(f32[512,16]{0,1:T(8,128)} %param.9) | copy-start | bytes 98308
  7.2 469.2 %all-gather.5.cloned.1.call-start = ((), (), s32[]{:S(2)}) async-start(), calls=%async_computation | async-start | bytes 69206016 | tf_op jit(solution)/shard_map/all_gather | solution.py:36
  11.8 8.1 copy-start.1
  11.8 77.1 %collective-permute-start = (f32[16,6,4096]{2,0,1:T(8,128)}, f32[16,6,4096]{2,0,1:T(8,128)}, u32[]{:S(2)}, u32[]{:S(2)}) collective-permute-start(f32[16,6,4096]{2,0,1:T(8,128)} %copy.22), channel_id=1, source_target_pairs={{1,0},{2,1},{3,2},{4,3},{5,4},{6,5},{7,6},{0,7},{9,8},{10,9},{11,1... | collective-permute-start | bytes 4718600 | tf_op jit(solution)/shard_map/ppermute | solution.py:27
  19.9 66.0 %collective-permute-start.1 = (f32[16,6,4096]{2,0,1:T(8,128)}, f32[16,6,4096]{2,0,1:T(8,128)}, u32[]{:S(2)}, u32[]{:S(2)}) collective-permute-start(f32[16,6,4096]{2,0,1:T(8,128)} %copy.23), channel_id=1, source_target_pairs={{0,1},{1,2},{2,3},{3,4},{4,5},{5,6},{6,7},{7,0},{8,9},{9,10},{10,1... | collective-permute-start | bytes 4718600 | tf_op jit(solution)/shard_map/ppermute | solution.py:25
  85.9 5.5 copy-start.5
  88.6 2.8 copy-start.4
  88.6 2.8 copy-start.6
  88.7 2.8 copy-start.7
  88.7 2.8 copy-start.8
  88.7 2.8 copy-start.9
  88.7 2.8 copy-start.10
  88.7 2.8 copy-start.11
  88.7 2.8 copy-start.12
  88.7 2.8 copy-start.13
  88.7 2.8 copy-start.14
  88.7 2.8 copy-start.15
  88.7 2.8 copy-start.16
  88.8 2.8 copy-start.17
  88.8 2.8 copy-start.18
  88.8 2.8 copy-start.19
  88.8 2.8 copy-start.20
  88.8 2.8 copy-start.21
  88.8 2.8 copy-start.22
  88.8 2.8 copy-start.23
  88.8 2.8 copy-start.24
  88.8 2.8 copy-start.25
  88.8 2.8 copy-start.26
  88.9 2.8 copy-start.27
  88.9 2.8 copy-start.28
  88.9 2.8 copy-start.29
  88.9 2.8 copy-start.30
  118.6 1.3 copy-start.2
  121.4 710.3 %all-gather.7.cloned.1.call-start = ((), (), s32[]{:S(2)}) async-start(), calls=%async_computation.1 | async-start | bytes 69206016 | tf_op jit(solution)/shard_map/all_gather | solution.py:36
  853.7 5.7 copy-start.3
Sparse Core Ops, SparseCore 0:
  121.5 354.8 all-gather.4
  478.2 353.4 all-gather.6
